TPU v7x, 512 devices: a whole 4x4x16 slice. The times are simulated.
512 devices in a mesh: view: 32 (over y_lo, z), band: 4 (over x), batch: 4 (over y_hi, core).
Axes of the slice: x: 4, y: 4 (y_hi: 2, y_lo: 2; y = y_hi * 2 + y_lo), z: 16, core: 2. Of those that a mesh axis runs over, the one named last changes fastest.
Arguments:
- images: bfloat16 [128, 32, 16, 768], P(('batch', 'view'), 'band'), parts along dimension 0, may hold values from -6 to 6
- frame_gain: float32 [768], replicated, may hold values from 0.5 to 2.5
- frame_qkv: bfloat16 [768, 1536], replicated, may hold values from -0.3 to 0.3
- frame_out: bfloat16 [512, 768], replicated, may hold values from -0.25 to 0.25
- row1_gain: float32 [768], replicated, may hold values from 0.5 to 2.5
- row1_qkv: bfloat16 [768, 1536], P('band'), may hold values from -0.3 to 0.3
- row1_out: bfloat16 [512, 768], P(None, 'band'), may hold values from -0.25 to 0.25
- row2_gain: float32 [768], replicated, may hold values from 0.5 to 2.5
- row2_qkv: bfloat16 [768, 1536], P('band'), may hold values from -0.3 to 0.3
- row2_out: bfloat16 [512, 768], P(None, 'band'), may hold values from -0.25 to 0.25
Outputs:
- refined: bfloat16 [128, 32, 16, 768], P(('batch', 'view'), 'band'), parts along dimension 0
There are 4 independent parts, one for each index of `batch`. A program takes and returns all parts, laid end to end along the dimension named above; an argument that names none is the same for every part. Nothing has to cross between parts.
All inputs are finite; a program needn't handle non-finite values.
Results may differ from a plain program's by a relative error of at most 0.02.
Values may be sent and summed in bfloat16 or wider, within the bound.
No kernel may reach another device: no remote copies, remote signals or barrier semaphores. Data moves between devices by JAX's collectives and lax.ppermute only.
A program may use at most 64 MiB of HBM per device.

v0:
```python
import math

import jax
import jax.numpy as jnp
from jax import lax
from jax.experimental import pallas as pl
from jax.experimental.pallas import tpu as pltpu
from jax.sharding import PartitionSpec as P


HEAD_DIM = 64
EPSILON = 1e-06
PAIR = 2 * HEAD_DIM
SCALE = HEAD_DIM ** (-0.5) * math.log2(math.e)
NORM_ROWS = 32
SOFTMAX_ROWS = 32


def project(all_ref, gain_ref, waits, weight_ref, normed_ref, kv_ref):
    chunks, tokens, width = all_ref.shape
    inner = kv_ref.shape[1] // 2
    gain = gain_ref[...].reshape(1, width)
    for chunk in range(chunks):
        for start in range(0, tokens, NORM_ROWS):
            values = all_ref[chunk, start : start + NORM_ROWS].astype(jnp.float32)
            factor = lax.rsqrt(jnp.mean(values * values, axis=-1, keepdims=True) + EPSILON)
            at = chunk * tokens + start
            normed_ref[at : at + NORM_ROWS, :] = (values * factor * gain).astype(jnp.bfloat16)
    for part in range(2):
        if waits:
            waits[1 + part]()
        kv_ref[:, part * inner : (part + 1) * inner] = jnp.dot(
            normed_ref[...],
            weight_ref[:, (1 + part) * inner : (2 + part) * inner],
            preferred_element_type=jnp.float32,
        ).astype(jnp.bfloat16)
    if waits:
        waits[0]()


def mixed(fence, read_normed, weight_ref, kv_ref, query_ref, score_ref, rounded_ref, inverse_ref, attended_ref):
    count = attended_ref.shape[0]
    inner = kv_ref.shape[1] // 2
    pairs = inner // PAIR

    @pl.when(fence)
    def _():
        first = lax.broadcasted_iota(jnp.int32, (count, PAIR), 1) < HEAD_DIM
        zeros = jnp.zeros((count, PAIR), jnp.bfloat16)
        queries = (
            jnp.dot(read_normed(), weight_ref[:, :inner], preferred_element_type=jnp.float32) * SCALE
        ).astype(jnp.bfloat16)
        for pair in range(pairs):
            query = queries[:, pair * PAIR : (pair + 1) * PAIR]
            query_ref[pair, :count] = jnp.where(first, query, zeros)
            query_ref[pair, count:] = jnp.where(first, zeros, query)

    def score(pair):
        score_ref[pair % 2] = lax.dot_general(
            query_ref[pair],
            kv_ref[:, pair * PAIR : (pair + 1) * PAIR],
            (((1,), (1,)), ((), ())),
            preferred_element_type=jnp.float32,
        )

    def weigh(pair):
        slot = pair % 2
        for start in range(0, 2 * count, SOFTMAX_ROWS):
            rows = slice(start, start + SOFTMAX_ROWS)
            scores = score_ref[slot, rows]
            weights = jnp.exp2(scores - jnp.max(scores, axis=-1, keepdims=True))
            total = jnp.sum(weights, axis=-1, keepdims=True)
            rounded_ref[slot, rows] = weights.astype(jnp.bfloat16)
            inverse_ref[slot, rows] = jnp.broadcast_to(1.0 / total, (SOFTMAX_ROWS, PAIR))

    def mix(pair):
        slot = pair % 2
        first = lax.broadcasted_iota(jnp.int32, (count, PAIR), 1) < HEAD_DIM
        result = inverse_ref[slot] * jnp.dot(
            rounded_ref[slot],
            kv_ref[:, inner + pair * PAIR : inner + (pair + 1) * PAIR],
            preferred_element_type=jnp.float32,
        )
        attended_ref[:, pair * PAIR : (pair + 1) * PAIR] = jnp.where(
            first, result[:count], result[count:]
        ).astype(jnp.bfloat16)

    for stage in range(pairs + 2):

        @pl.when(fence)
        def _(stage=stage):
            if stage < pairs:
                score(stage)
            if 0 <= stage - 1 < pairs:
                weigh(stage - 1)
            if 0 <= stage - 2:
                mix(stage - 2)


def mixing_scratch(count, keys, inner):
    pairs = inner // PAIR
    return [
        pltpu.VMEM((pairs, 2 * count, PAIR), jnp.bfloat16),
        pltpu.VMEM((2, 2 * count, keys), jnp.float32),
        pltpu.VMEM((2, 2 * count, keys), jnp.bfloat16),
        pltpu.VMEM((2, 2 * count, PAIR), jnp.float32),
        pltpu.VMEM((count, inner), jnp.bfloat16),
    ]


def chunk_of(normed_ref, own, tokens):
    return normed_ref[pl.ds(pl.multiple_of(own * tokens, tokens), tokens), :]


def started(copies):
    for copy in copies:
        copy.start()

    def wait():
        for copy in copies:
            copy.wait()

    return wait


def pack_body(*refs):
    shards, nears, sems = refs[:4], refs[4:6], refs[6]
    columns = shards[0].shape[1]
    copies = []
    for layer in range(2):
        qkv, out = shards[2 * layer : 2 * layer + 2]
        copies.append(
            pltpu.make_async_copy(qkv, nears[layer].at[:, :columns], sems.at[2 * layer])
        )
        copies.append(
            pltpu.make_async_copy(out, nears[layer].at[:, columns:], sems.at[2 * layer + 1])
        )
    started(copies)()


def pack_layer(shards):
    qkv, out = shards[:2]
    return pl.pallas_call(
        pack_body,
        out_shape=(
            jax.ShapeDtypeStruct((qkv.shape[0], qkv.shape[1] + out.shape[1]), jnp.bfloat16),
        )
        * 2,
        in_specs=[pl.BlockSpec(memory_space=pltpu.HBM)] * 4,
        out_specs=(pl.BlockSpec(memory_space=pltpu.VMEM),) * 2,
        scratch_shapes=[pltpu.SemaphoreType.DMA((4,))],
        compiler_params=pltpu.CompilerParams(vmem_limit_bytes=4 << 20),
        name="pack",
    )(*kept(*shards))


def frame_body(
    all_ref,
    gain_ref,
    weight_ref,
    out_ref,
    result_ref,
    mix_ref,
    normed_ref,
    kv_ref,
    sem,
    *mixing,
):
    band = lax.axis_index("band")
    mix = started([pltpu.make_async_copy(out_ref, mix_ref, sem)])
    project(all_ref, gain_ref, None, weight_ref, normed_ref, kv_ref)
    _, tokens, _ = all_ref.shape
    mixed(band >= 0, lambda: chunk_of(normed_ref, band, tokens), weight_ref, kv_ref, *mixing)
    mix()
    update = jnp.dot(mixing[-1][...], mix_ref[...], preferred_element_type=jnp.float32)
    result_ref[...] = (all_ref[band].astype(jnp.float32) + update).astype(jnp.bfloat16)


def kept(*arrays):
    return [pltpu.with_memory_space_constraint(array, pltpu.HBM) for array in arrays]


def frame_layer(everything, gain, qkv, out):
    chunks, tokens, width = everything.shape
    inner = out.shape[0]
    count = chunks * tokens
    vmem = pl.BlockSpec(memory_space=pltpu.VMEM)
    return pl.pallas_call(
        frame_body,
        out_shape=jax.ShapeDtypeStruct((tokens, width), jnp.bfloat16),
        in_specs=[vmem] * 3 + [pl.BlockSpec(memory_space=pltpu.HBM)],
        out_specs=vmem,
        scratch_shapes=[
            pltpu.VMEM((inner, width), jnp.bfloat16),
            pltpu.VMEM((count, width), jnp.bfloat16),
            pltpu.VMEM((count, 2 * inner), jnp.bfloat16),
            pltpu.SemaphoreType.DMA,
        ]
        + mixing_scratch(tokens, count, inner),
        compiler_params=pltpu.CompilerParams(vmem_limit_bytes=20 << 20),
        cost_estimate=estimate(chunks, tokens, width, inner),
        name="frame",
    )(everything, gain, qkv, *kept(out))


def estimate(chunks, tokens, width, inner):
    count = chunks * tokens
    return pl.CostEstimate(
        flops=4 * count * width * inner + 4 * tokens * width * inner + 4 * tokens * count * inner,
        bytes_accessed=2 * (count * width + 4 * width * inner),
        transcendentals=tokens * count * inner // HEAD_DIM,
    )


def assembled(parts, weight_ref, sems, band, bands, core):
    inner = parts[1].shape[1]
    rows = parts[1].shape[0]
    target = [
        pl.ds(pl.multiple_of(lax.rem(band + step, bands) * rows, rows), rows)
        for step in (0, bands - 1 + 2 * core, 2, 1 + 2 * core)
    ]
    waits = {}
    for order, part in enumerate((1, 2, 0, 3)):
        columns = slice(part * inner, (part + 1) * inner)
        sources = (parts[1] if part == 3 else parts[0].at[:, columns],)
        sources += tuple(ref.at[:, columns] for ref in parts[2:])
        waits[part] = started(
            [
                pltpu.make_async_copy(source, weight_ref.at[goal, columns], sems.at[order, index])
                for index, (source, goal) in enumerate(zip(sources, target))
            ]
        )
    return waits


def rows_body(all_ref, gain1_ref, gain2_ref, *refs):
    parts1, parts2, refs = refs[:5], refs[5:10], refs[10:]
    result_ref, weight1_ref, weight2_ref, normed_ref, kv_ref, stream_ref, sems = refs[:7]
    mixing1, mixing2 = refs[7:12], refs[12:]
    chunks = all_ref.shape[0]
    inner = kv_ref.shape[1] // 2
    bands = lax.axis_size("band")
    band = lax.axis_index("band")
    core = lax.rem(lax.axis_index("batch"), 2)
    view = lax.axis_index("view")
    deep = lax.axis_size("view") // 2
    left = lax.rem(view, 2)
    own = jnp.where(view < deep, left, chunks - 1 - left)
    contract = (((1,), (1,)), ((), ()))
    waits1 = assembled(parts1, weight1_ref, sems.at[0], band, bands, core)
    waits2 = assembled(parts2, weight2_ref, sems.at[1], band, bands, core)
    project(all_ref, gain1_ref, waits1, weight1_ref, normed_ref, kv_ref)
    _, tokens, _ = all_ref.shape
    mixed(band >= 0, lambda: normed_ref[...], weight1_ref, kv_ref, *mixing1)
    waits1[3]()
    update = lax.dot_general(
        mixing1[-1][...], weight1_ref[:, 3 * inner :], contract, preferred_element_type=jnp.float32
    )
    for chunk in range(chunks):
        stream_ref[chunk] = (
            all_ref[chunk].astype(jnp.float32) + update[chunk * tokens : (chunk + 1) * tokens]
        ).astype(jnp.bfloat16)
    for part in range(4):
        waits2[part]()
    project(stream_ref, gain2_ref, None, weight2_ref, normed_ref, kv_ref)
    mixed(band >= 0, lambda: chunk_of(normed_ref, own, tokens), weight2_ref, kv_ref, *mixing2)
    update = lax.dot_general(
        mixing2[-1][...], weight2_ref[:, 3 * inner :], contract, preferred_element_type=jnp.float32
    )
    result_ref[...] = (stream_ref[own].astype(jnp.float32) + update).astype(jnp.bfloat16)


def rows_layer(everything, gain1, gain2, weights):
    chunks, tokens, width = everything.shape
    inner = weights[1].shape[1]
    count = chunks * tokens
    vmem = pl.BlockSpec(memory_space=pltpu.VMEM)
    hbm = pl.BlockSpec(memory_space=pltpu.HBM)
    return pl.pallas_call(
        rows_body,
        out_shape=jax.ShapeDtypeStruct((tokens, width), jnp.bfloat16),
        in_specs=[vmem] * 3 + [hbm] * 2 + [pl.BlockSpec(memory_space=pl.ANY)] * 3 + [hbm] * 5,
        out_specs=vmem,
        scratch_shapes=[
            pltpu.VMEM((width, 4 * inner), jnp.bfloat16),
            pltpu.VMEM((width, 4 * inner), jnp.bfloat16),
            pltpu.VMEM((count, width), jnp.bfloat16),
            pltpu.VMEM((count, 2 * inner), jnp.bfloat16),
            pltpu.VMEM((chunks, tokens, width), jnp.bfloat16),
            pltpu.SemaphoreType.DMA((2, 4, 4)),
        ]
        + mixing_scratch(count, count, inner)
        + mixing_scratch(tokens, count, inner),
        compiler_params=pltpu.CompilerParams(vmem_limit_bytes=32 << 20),
        cost_estimate=estimate(chunks, tokens, width, inner),
        name="rows",
    )(everything, gain1, gain2, *kept(*weights[:2]), *weights[2:5], *kept(*weights[5:]))


def exchanged(stream, rows, groups):
    tokens, width = stream.shape
    return lax.all_to_all(
        stream.reshape(rows, tokens // rows, width),
        "view",
        split_axis=0,
        concat_axis=0,
        tiled=True,
        axis_index_groups=groups,
    ).reshape(tokens, width)


def layers(
    images,
    frame_gain,
    frame_qkv,
    frame_out,
    row1_gain,
    row1_qkv,
    row1_out,
    row2_gain,
    row2_qkv,
    row2_out,
):
    _, row_count, col_count, width = images.shape
    tokens = row_count * col_count
    views = lax.axis_size("view")
    bands = lax.axis_size("band")
    batches = lax.axis_size("batch")
    share = views // row_count
    near = 2
    deep = views // near
    side = share // near
    spread = [
        [y * deep + h * side + l for h in range(row_count)] for y in range(near) for l in range(side)
    ]
    ring = [
        [h * side + l for l in range(side)] + [deep + h * side + l for l in reversed(range(side))]
        for h in range(row_count)
    ]
    siblings = [(i, i ^ 1) for i in range(batches)]
    turn = [
        (b * batches + c, ((b + 1 - 2 * (c % 2)) % bands) * batches + c)
        for b in range(bands)
        for c in range(batches)
    ]

    shards = (row1_qkv, row1_out.T, row2_qkv, row2_out.T)
    everything = lax.all_gather(images.reshape(tokens, width), "band", axis=0, tiled=False)
    everything, nears = lax.optimization_barrier((everything, pack_layer(shards)))

    both = ("band", "batch")
    nears = [lax.ppermute(near, both, turn) for near in nears]
    stream = frame_layer(everything, frame_gain, frame_qkv, frame_out)
    stream = exchanged(stream, row_count, spread)
    fars = [lax.ppermute(near, both, turn) for near in nears]
    others = [lax.ppermute(near, "batch", siblings) for near in nears]
    gain1 = row1_gain.reshape(1, width)
    gain2 = row2_gain.reshape(1, width)
    everything = lax.all_gather(stream, "view", axis=0, tiled=False, axis_index_groups=ring)
    stream = rows_layer(
        everything, gain1, gain2, (*shards[:2], nears[0], fars[0], others[0], *shards[2:], nears[1], fars[1], others[1])
    )
    stream = exchanged(stream, row_count, spread)
    return stream.reshape(images.shape)


def solution(mesh):
    in_specs = (
        P(("batch", "view"), "band", None, None),
        P(),
        P(),
        P(),
        P(),
        P("band", None),
        P(None, "band"),
        P(),
        P("band", None),
        P(None, "band"),
    )
    out_specs = P(("batch", "view"), "band", None, None)
    return jax.shard_map(layers, mesh=mesh, in_specs=in_specs, out_specs=out_specs, check_vma=False)
```

profile of v0, /device:TPU:30, one launch (start us, length us, event | category | flops | bytes accessed | tf_op | source)
XLA Modules:
  0.0 105.0 jit_solution(4249486355387746048)
XLA Ops:
  0.0 0.0 copy-start
  0.0 0.0 copy-start.1
  0.0 14.4 %all_gather.6.all_ref = bf16[4,128,768]{2,1,0:T(8,128)(2,1)S(1)} all-gather(bf16[1,128,768]{2,1,0:T(8,128)(2,1)} %bitcast.14), channel_id=1, replica_groups=mesh['view'=32,'band'=4,'batch'=4] {'band'}, dimensions={0}, use_global_device_ids=true | all-gather | bytes 983040 | tf_op jit(solution)/shard_map/all_gather | solution.py:348
  14.4 1.4 %pack.1 = (bf16[192,2048]{1,0:T(8,128)(2,1)S(1)}, bf16[192,2048]{1,0:T(8,128)(2,1)S(1)}) custom-call(bf16[192,1536]{1,0:T(8,128)(2,1)} %refs_0_.3, bf16[192,512]{1,0:T(8,128)(2,1)} %bitcast.10, bf16[192,1536]{1,0:T(8,128)(2,1)} %refs_5_.1, bf16[192,512]{1,0:T(8,128)(2,1)} %bitcast.12), custom_call_target="tpu_custom_call" | custom-call | tf_op jit(solution)/shard_map/pack/pallas_call | solution.py:143
  15.8 0.0 copy-start.2
  15.8 0.0 copy-start.3
  15.8 2.0 %collective-permute-start = (bf16[192,2048]{1,0:T(8,128)(2,1)S(1)}, bf16[192,2048]{1,0:T(8,128)(2,1)S(1)}, u32[]{:S(2)}, u32[]{:S(2)}) collective-permute-start(bf16[192,2048]{1,0:T(8,128)(2,1)S(1)} %get-tuple-element.13), channel_id=1, source_target_pairs={{0,4},{1,13},{2,6},{3,15},{4,8},{5,1},{6,10},{7,3},{8,12},{9,5},{1... | collective-permute-start | bytes 2359304 | tf_op jit(solution)/shard_map/ppermute | solution.py:352
  17.8 3.8 %collective-permute-start.3 = (bf16[192,2048]{1,0:T(8,128)(2,1)S(1)}, bf16[192,2048]{1,0:T(8,128)(2,1)}, u32[]{:S(2)}, u32[]{:S(2)}) collective-permute-start(bf16[192,2048]{1,0:T(8,128)(2,1)S(1)} %get-tuple-element.14), channel_id=1, source_target_pairs={{0,4},{1,13},{2,6},{3,15},{4,8},{5,1},{6,10},{7,3},{8,12},{9,5},{1... | collective-permute-start | bytes 2359304 | tf_op jit(solution)/shard_map/ppermute | solution.py:352
  21.7 0.0 copy-done
  21.7 0.0 copy-done.1
  21.7 3.2 %frame.1 = bf16[128,768]{1,0:T(8,128)(2,1)} custom-call(bf16[4,128,768]{2,1,0:T(8,128)(2,1)S(1)} %all_gather.6.all_ref, f32[768]{0:T(1024)S(1)} %copy-done.1, bf16[768,1536]{1,0:T(8,128)(2,1)S(1)} %copy-done, bf16[512,768]{1,0:T(8,128)(2,1)} %out_ref.1), custom_call_target="tpu_custom_call" | custom-call | flops 1140850688 | bytes 3932160 | tf_op jit(solution)/shard_map/frame/pallas_call | solution.py:188
  24.8 15.1 %all-to-all-start = ((bf16[8,16,768]{2,1,0:T(8,128)(2,1)}), bf16[8,16,768]{2,1,0:T(8,128)(2,1)S(1)}, u32[]{:S(2)}, u32[]{:S(2)}) async-start(bf16[8,16,768]{2,1,0:T(8,128)(2,1)} %bitcast.3), calls=%async_computation | async-start | bytes 393216 | tf_op jit(solution)/shard_map/all_to_all | solution.py:302
  39.9 0.0 collective-permute-done.refs_2_
  39.9 1.9 %collective-permute-start.2 = (bf16[192,2048]{1,0:T(8,128)(2,1)S(1)}, bf16[192,2048]{1,0:T(8,128)(2,1)S(1)}, u32[]{:S(2)}, u32[]{:S(2)}) collective-permute-start(bf16[192,2048]{1,0:T(8,128)(2,1)S(1)} %collective-permute-done.refs_2_), channel_id=1, source_target_pairs={{0,1},{1,0},{2,3},{3,2},{4,5},{5,4},{6,7},{7,6},{8,9},{9,8},{10,11... | collective-permute-start | bytes 2359304 | tf_op jit(solution)/shard_map/ppermute | solution.py:356
  41.9 1.9 %collective-permute-start.1 = (bf16[192,2048]{1,0:T(8,128)(2,1)S(1)}, bf16[192,2048]{1,0:T(8,128)(2,1)S(1)}, u32[]{:S(2)}, u32[]{:S(2)}) collective-permute-start(bf16[192,2048]{1,0:T(8,128)(2,1)S(1)} %collective-permute-done.refs_2_), channel_id=1, source_target_pairs={{0,4},{1,13},{2,6},{3,15},{4,8},{5,1},{6,10},{7,3},{8,12},{9,5},{1... | collective-permute-start | bytes 2359304 | tf_op jit(solution)/shard_map/ppermute | solution.py:355
  43.8 0.0 collective-permute-done.3.refs_7_
  43.8 2.4 %collective-permute-start.5 = (bf16[192,2048]{1,0:T(8,128)(2,1)}, bf16[192,2048]{1,0:T(8,128)(2,1)}, u32[]{:S(2)}, u32[]{:S(2)}) collective-permute-start(bf16[192,2048]{1,0:T(8,128)(2,1)} %collective-permute-done.3.refs_7_), channel_id=1, source_target_pairs={{0,1},{1,0},{2,3},{3,2},{4,5},{5,4},{6,7},{7,6},{8,9},{9,8},{10,11... | collective-permute-start | bytes 2359304 | tf_op jit(solution)/shard_map/ppermute | solution.py:356
  46.2 4.9 %collective-permute-start.4 = (bf16[192,2048]{1,0:T(8,128)(2,1)}, bf16[192,2048]{1,0:T(8,128)(2,1)}, u32[]{:S(2)}, u32[]{:S(2)}) collective-permute-start(bf16[192,2048]{1,0:T(8,128)(2,1)} %collective-permute-done.3.refs_7_), channel_id=1, source_target_pairs={{0,4},{1,13},{2,6},{3,15},{4,8},{5,1},{6,10},{7,3},{8,12},{9,5},{1... | collective-permute-start | bytes 2359304 | tf_op jit(solution)/shard_map/ppermute | solution.py:355
  51.1 0.0 copy-done.2
  51.1 0.0 copy-done.3
  51.1 4.7 %all-to-all-done = bf16[8,16,768]{2,1,0:T(8,128)(2,1)S(1)} async-done(((bf16[8,16,768]{2,1,0:T(8,128)(2,1)}), bf16[8,16,768]{2,1,0:T(8,128)(2,1)S(1)}, u32[]{:S(2)}, u32[]{:S(2)}) %all-to-all-start) | async-done | bytes 196640 | tf_op jit(solution)/shard_map/all_to_all | solution.py:302
  55.8 10.9 %all_gather.7.all_ref = bf16[4,128,768]{2,1,0:T(8,128)(2,1)S(1)} all-gather(bf16[1,128,768]{2,1,0:T(8,128)(2,1)S(1)} %bitcast.9), channel_id=1, replica_groups={{0,16,272,256},{32,48,304,288},{64,80,336,320},{96,112,368,352},{128,14..., dimensions={0}, use_global_device_ids=true | all-gather | bytes 983040 | tf_op jit(solution)/shard_map/all_gather | solution.py:359
  66.7 0.0 collective-permute-done.2.refs_4_
  66.7 0.0 collective-permute-done.1.refs_3_
  66.7 0.0 collective-permute-done.5.refs_9_
  66.7 0.0 collective-permute-done.4.refs_8_
  66.7 8.9 %rows.1 = bf16[128,768]{1,0:T(8,128)(2,1)S(1)} custom-call(bf16[4,128,768]{2,1,0:T(8,128)(2,1)S(1)} %all_gather.7.all_ref, f32[1,768]{1,0:T(1,128)S(1)} %reshape.13.gain1_ref, f32[1,768]{1,0:T(1,128)S(1)} %reshape.14.gain2_ref, bf16[192,1536]{1,0:T(8,128)(2,1)} %refs_0_.3, bf16[192,512]{1,0:T(8,128)(2,1)} %bitcast.11, ...), custom_call_target="tpu_custom_call" | custom-call | flops 1140850688 | bytes 3932160 | tf_op jit(solution)/shard_map/rows/pallas_call | solution.py:279
  75.6 28.7 %all_to_all.10 = bf16[8,16,768]{2,1,0:T(8,128)(2,1)S(1)} all-to-all(bf16[8,16,768]{2,1,0:T(8,128)(2,1)S(1)} %bitcast.7), channel_id=1, replica_groups={{0,32,64,96,128,160,192,224},{16,48,80,112,144,176,208,240},{256,288,32..., dimensions={0} | all-to-all | bytes 393216 | tf_op jit(solution)/shard_map/all_to_all | solution.py:302
  104.3 0.7 copy.12
  (2 shorter events, 0.0 us)
Async XLA Ops:
  0.0 21.7 %copy-start = (bf16[768,1536]{1,0:T(8,128)(2,1)S(1)}, bf16[768,1536]{1,0:T(8,128)(2,1)}, u32[]{:S(2)}) copy-start(bf16[768,1536]{1,0:T(8,128)(2,1)} %weight_ref.1) | copy-start | bytes 7077892
  0.0 21.7 %copy-start.1 = (f32[768]{0:T(1024)S(1)}, f32[768]{0:T(1024)}, u32[]{:S(2)}) copy-start(f32[768]{0:T(1024)} %gain_ref.1) | copy-start | bytes 9220
  15.8 35.3 %copy-start.2 = (f32[768]{0:T(1024)S(1)}, f32[768]{0:T(1024)}, u32[]{:S(2)}) copy-start(f32[768]{0:T(1024)} %param.14) | copy-start | bytes 9220
  15.8 35.3 %copy-start.3 = (f32[768]{0:T(1024)S(1)}, f32[768]{0:T(1024)}, u32[]{:S(2)}) copy-start(f32[768]{0:T(1024)} %param.17) | copy-start | bytes 9220
  15.8 24.1 %collective-permute-start = (bf16[192,2048]{1,0:T(8,128)(2,1)S(1)}, bf16[192,2048]{1,0:T(8,128)(2,1)S(1)}, u32[]{:S(2)}, u32[]{:S(2)}) collective-permute-start(bf16[192,2048]{1,0:T(8,128)(2,1)S(1)} %get-tuple-element.13), channel_id=1, source_target_pairs={{0,4},{1,13},{2,6},{3,15},{4,8},{5,1},{6,10},{7,3},{8,12},{9,5},{1... | collective-permute-start | bytes 2359304 | tf_op jit(solution)/shard_map/ppermute | solution.py:352
  17.8 26.0 %collective-permute-start.3 = (bf16[192,2048]{1,0:T(8,128)(2,1)S(1)}, bf16[192,2048]{1,0:T(8,128)(2,1)}, u32[]{:S(2)}, u32[]{:S(2)}) collective-permute-start(bf16[192,2048]{1,0:T(8,128)(2,1)S(1)} %get-tuple-element.14), channel_id=1, source_target_pairs={{0,4},{1,13},{2,6},{3,15},{4,8},{5,1},{6,10},{7,3},{8,12},{9,5},{1... | collective-permute-start | bytes 2359304 | tf_op jit(solution)/shard_map/ppermute | solution.py:352
  24.8 31.0 %all-to-all-start = ((bf16[8,16,768]{2,1,0:T(8,128)(2,1)}), bf16[8,16,768]{2,1,0:T(8,128)(2,1)S(1)}, u32[]{:S(2)}, u32[]{:S(2)}) async-start(bf16[8,16,768]{2,1,0:T(8,128)(2,1)} %bitcast.3), calls=%async_computation | async-start | bytes 393216 | tf_op jit(solution)/shard_map/all_to_all | solution.py:302
  39.9 26.8 %collective-permute-start.2 = (bf16[192,2048]{1,0:T(8,128)(2,1)S(1)}, bf16[192,2048]{1,0:T(8,128)(2,1)S(1)}, u32[]{:S(2)}, u32[]{:S(2)}) collective-permute-start(bf16[192,2048]{1,0:T(8,128)(2,1)S(1)} %collective-permute-done.refs_2_), channel_id=1, source_target_pairs={{0,1},{1,0},{2,3},{3,2},{4,5},{5,4},{6,7},{7,6},{8,9},{9,8},{10,11... | collective-permute-start | bytes 2359304 | tf_op jit(solution)/shard_map/ppermute | solution.py:356
  41.9 24.8 %collective-permute-start.1 = (bf16[192,2048]{1,0:T(8,128)(2,1)S(1)}, bf16[192,2048]{1,0:T(8,128)(2,1)S(1)}, u32[]{:S(2)}, u32[]{:S(2)}) collective-permute-start(bf16[192,2048]{1,0:T(8,128)(2,1)S(1)} %collective-permute-done.refs_2_), channel_id=1, source_target_pairs={{0,4},{1,13},{2,6},{3,15},{4,8},{5,1},{6,10},{7,3},{8,12},{9,5},{1... | collective-permute-start | bytes 2359304 | tf_op jit(solution)/shard_map/ppermute | solution.py:355
  43.8 22.9 %collective-permute-start.5 = (bf16[192,2048]{1,0:T(8,128)(2,1)}, bf16[192,2048]{1,0:T(8,128)(2,1)}, u32[]{:S(2)}, u32[]{:S(2)}) collective-permute-start(bf16[192,2048]{1,0:T(8,128)(2,1)} %collective-permute-done.3.refs_7_), channel_id=1, source_target_pairs={{0,1},{1,0},{2,3},{3,2},{4,5},{5,4},{6,7},{7,6},{8,9},{9,8},{10,11... | collective-permute-start | bytes 2359304 | tf_op jit(solution)/shard_map/ppermute | solution.py:356
  46.2 20.5 %collective-permute-start.4 = (bf16[192,2048]{1,0:T(8,128)(2,1)}, bf16[192,2048]{1,0:T(8,128)(2,1)}, u32[]{:S(2)}, u32[]{:S(2)}) collective-permute-start(bf16[192,2048]{1,0:T(8,128)(2,1)} %collective-permute-done.3.refs_7_), channel_id=1, source_target_pairs={{0,4},{1,13},{2,6},{3,15},{4,8},{5,1},{6,10},{7,3},{8,12},{9,5},{1... | collective-permute-start | bytes 2359304 | tf_op jit(solution)/shard_map/ppermute | solution.py:355
where the time goes:
time: 105 us
  blocking collectives  53.9 us (51%)
  starting transfers between devices  32.1 us (31%)
  Pallas kernels  13.4 us (13%)
  waiting for transfers between devices  4.69 us (4%)
    all_to_all x1, blocking collectives, exchanged(): lax.all_to_all(stream.reshape(rows, tokens // rows, width), 'view', split...  28.7 us
    all_to_all x1, starting transfers between devices, exchanged(): lax.all_to_all(stream.reshape(rows, tokens // rows, width), 'view', split...  15.1 us
    all_gather x1, blocking collectives, layers(): lax.all_gather(images.reshape(tokens, width), 'band', axis=0, tiled=False)  14.4 us
    all_gather x1, blocking collectives, layers(): lax.all_gather(stream, 'view', axis=0, tiled=False, axis_index_groups=ring)  10.9 us
    pallas_call x1, Pallas kernels, rows_layer(): pl.pallas_call(rows_body, out_shape=jax.ShapeDtypeStruct((tokens, width),...  8.91 us
    ppermute x2, starting transfers between devices, layers(): fars = [lax.ppermute(near, both, turn) for near in nears]  6.78 us
    ppermute x2, starting transfers between devices, layers(): nears = [lax.ppermute(near, both, turn) for near in nears]  5.84 us
    all_to_all x1, waiting for transfers between devices, exchanged(): lax.all_to_all(stream.reshape(rows, tokens // rows, width), 'view', split...  4.68 us
  transfers between devices with their start and end apart: 7, of which 1 were waited for; matrix products, arithmetic and copies ran while one was open for 0% of the time, Pallas kernels for 3%

commit v1 on v0

--- a/solution.py
+++ b/solution.py
@@ -13,6 +13,7 @@
 PAIR = 2 * HEAD_DIM
 SCALE = HEAD_DIM ** (-0.5) * math.log2(math.e)
 NORM_ROWS = 32
+PACK_PARTS = 4
 SOFTMAX_ROWS = 32
 
 
@@ -129,12 +130,15 @@
     copies = []
     for layer in range(2):
         qkv, out = shards[2 * layer : 2 * layer + 2]
-        copies.append(
-            pltpu.make_async_copy(qkv, nears[layer].at[:, :columns], sems.at[2 * layer])
-        )
-        copies.append(
-            pltpu.make_async_copy(out, nears[layer].at[:, columns:], sems.at[2 * layer + 1])
-        )
+        rows = qkv.shape[0] // PACK_PARTS
+        for part in range(PACK_PARTS):
+            at = slice(part * rows, (part + 1) * rows)
+            for index, (source, goal) in enumerate(
+                ((qkv, nears[layer].at[at, :columns]), (out, nears[layer].at[at, columns:]))
+            ):
+                copies.append(
+                    pltpu.make_async_copy(source.at[at, :], goal, sems.at[layer, part, index])
+                )
     started(copies)()
 
 
@@ -148,7 +152,7 @@
         * 2,
         in_specs=[pl.BlockSpec(memory_space=pltpu.HBM)] * 4,
         out_specs=(pl.BlockSpec(memory_space=pltpu.VMEM),) * 2,
-        scratch_shapes=[pltpu.SemaphoreType.DMA((4,))],
+        scratch_shapes=[pltpu.SemaphoreType.DMA((2, PACK_PARTS, 2))],
         compiler_params=pltpu.CompilerParams(vmem_limit_bytes=4 << 20),
         name="pack",
     )(*kept(*shards))

time: 105 us -> 106 us (level)
  the two profiles are of different devices: /device:TPU:30 before, /device:TPU:6 now
where the time goes in v1:
time: 106 us; the launch traced here: 105 us
  blocking collectives  56.4 us (53%)
  starting transfers between devices  29.6 us (28%)
  Pallas kernels  13.6 us (13%)
  waiting for transfers between devices  4.7 us (4%)
    all_to_all x1, blocking collectives, exchanged(): lax.all_to_all(stream.reshape(rows, tokens // rows, width), 'view', split...  28.7 us
    all_gather x1, blocking collectives, layers(): lax.all_gather(images.reshape(tokens, width), 'band', axis=0, tiled=False)  16.8 us
    all_to_all x1, starting transfers between devices, exchanged(): lax.all_to_all(stream.reshape(rows, tokens // rows, width), 'view', split...  12 us
    all_gather x1, blocking collectives, layers(): lax.all_gather(stream, 'view', axis=0, tiled=False, axis_index_groups=ring)  10.9 us
    pallas_call x1, Pallas kernels, rows_layer(): pl.pallas_call(rows_body, out_shape=jax.ShapeDtypeStruct((tokens, width),...  8.91 us
    ppermute x2, starting transfers between devices, layers(): fars = [lax.ppermute(near, both, turn) for near in nears]  6.77 us
    ppermute x2, starting transfers between devices, layers(): nears = [lax.ppermute(near, both, turn) for near in nears]  6.47 us
    all_to_all x1, waiting for transfers between devices, exchanged(): lax.all_to_all(stream.reshape(rows, tokens // rows, width), 'view', split...  4.68 us
  transfers between devices with their start and end apart: 7, of which 1 were waited for; matrix products, arithmetic and copies ran while one was open for 0% of the time, Pallas kernels for 3%

profile of v1, /device:TPU:6, one launch (start us, length us, event | category | flops | bytes accessed | tf_op | source)
XLA Modules:
  0.0 105.2 jit_solution(374405889168802219)
XLA Ops:
  0.0 0.0 copy-start
  0.0 0.0 copy-start.1
  0.0 16.8 %all_gather.6.all_ref = bf16[4,128,768]{2,1,0:T(8,128)(2,1)S(1)} all-gather(bf16[1,128,768]{2,1,0:T(8,128)(2,1)} %bitcast.14), channel_id=1, replica_groups=mesh['view'=32,'band'=4,'batch'=4] {'band'}, dimensions={0}, use_global_device_ids=true | all-gather | bytes 983040 | tf_op jit(solution)/shard_map/all_gather | solution.py:352
  16.9 1.6 %pack.1 = (bf16[192,2048]{1,0:T(8,128)(2,1)S(1)}, bf16[192,2048]{1,0:T(8,128)(2,1)S(1)}) custom-call(bf16[192,1536]{1,0:T(8,128)(2,1)} %refs_0_.3, bf16[192,512]{1,0:T(8,128)(2,1)} %bitcast.10, bf16[192,1536]{1,0:T(8,128)(2,1)} %refs_5_.1, bf16[192,512]{1,0:T(8,128)(2,1)} %bitcast.12), custom_call_target="tpu_custom_call" | custom-call | tf_op jit(solution)/shard_map/pack/pallas_call | solution.py:147
  18.4 0.0 copy-start.2
  18.4 0.0 copy-start.3
  18.5 4.6 %collective-permute-start = (bf16[192,2048]{1,0:T(8,128)(2,1)S(1)}, bf16[192,2048]{1,0:T(8,128)(2,1)S(1)}, u32[]{:S(2)}, u32[]{:S(2)}) collective-permute-start(bf16[192,2048]{1,0:T(8,128)(2,1)S(1)} %get-tuple-element.13), channel_id=1, source_target_pairs={{0,4},{1,13},{2,6},{3,15},{4,8},{5,1},{6,10},{7,3},{8,12},{9,5},{1... | collective-permute-start | bytes 2359304 | tf_op jit(solution)/shard_map/ppermute | solution.py:356
  23.0 1.9 %collective-permute-start.3 = (bf16[192,2048]{1,0:T(8,128)(2,1)S(1)}, bf16[192,2048]{1,0:T(8,128)(2,1)}, u32[]{:S(2)}, u32[]{:S(2)}) collective-permute-start(bf16[192,2048]{1,0:T(8,128)(2,1)S(1)} %get-tuple-element.14), channel_id=1, source_target_pairs={{0,4},{1,13},{2,6},{3,15},{4,8},{5,1},{6,10},{7,3},{8,12},{9,5},{1... | collective-permute-start | bytes 2359304 | tf_op jit(solution)/shard_map/ppermute | solution.py:356
  24.9 0.0 copy-done
  25.0 0.0 copy-done.1
  25.0 3.2 %frame.1 = bf16[128,768]{1,0:T(8,128)(2,1)} custom-call(bf16[4,128,768]{2,1,0:T(8,128)(2,1)S(1)} %all_gather.6.all_ref, f32[768]{0:T(1024)S(1)} %copy-done.1, bf16[768,1536]{1,0:T(8,128)(2,1)S(1)} %copy-done, bf16[512,768]{1,0:T(8,128)(2,1)} %out_ref.1), custom_call_target="tpu_custom_call" | custom-call | flops 1140850688 | bytes 3932160 | tf_op jit(solution)/shard_map/frame/pallas_call | solution.py:192
  28.1 12.0 %all-to-all-start = ((bf16[8,16,768]{2,1,0:T(8,128)(2,1)}), bf16[8,16,768]{2,1,0:T(8,128)(2,1)S(1)}, u32[]{:S(2)}, u32[]{:S(2)}) async-start(bf16[8,16,768]{2,1,0:T(8,128)(2,1)} %bitcast.3), calls=%async_computation | async-start | bytes 393216 | tf_op jit(solution)/shard_map/all_to_all | solution.py:306
  40.2 0.0 collective-permute-done.refs_2_
  40.2 1.9 %collective-permute-start.2 = (bf16[192,2048]{1,0:T(8,128)(2,1)S(1)}, bf16[192,2048]{1,0:T(8,128)(2,1)S(1)}, u32[]{:S(2)}, u32[]{:S(2)}) collective-permute-start(bf16[192,2048]{1,0:T(8,128)(2,1)S(1)} %collective-permute-done.refs_2_), channel_id=1, source_target_pairs={{0,1},{1,0},{2,3},{3,2},{4,5},{5,4},{6,7},{7,6},{8,9},{9,8},{10,11... | collective-permute-start | bytes 2359304 | tf_op jit(solution)/shard_map/ppermute | solution.py:360
  42.1 1.9 %collective-permute-start.1 = (bf16[192,2048]{1,0:T(8,128)(2,1)S(1)}, bf16[192,2048]{1,0:T(8,128)(2,1)S(1)}, u32[]{:S(2)}, u32[]{:S(2)}) collective-permute-start(bf16[192,2048]{1,0:T(8,128)(2,1)S(1)} %collective-permute-done.refs_2_), channel_id=1, source_target_pairs={{0,4},{1,13},{2,6},{3,15},{4,8},{5,1},{6,10},{7,3},{8,12},{9,5},{1... | collective-permute-start | bytes 2359304 | tf_op jit(solution)/shard_map/ppermute | solution.py:359
  44.0 0.0 collective-permute-done.3.refs_7_
  44.0 2.4 %collective-permute-start.5 = (bf16[192,2048]{1,0:T(8,128)(2,1)}, bf16[192,2048]{1,0:T(8,128)(2,1)}, u32[]{:S(2)}, u32[]{:S(2)}) collective-permute-start(bf16[192,2048]{1,0:T(8,128)(2,1)} %collective-permute-done.3.refs_7_), channel_id=1, source_target_pairs={{0,1},{1,0},{2,3},{3,2},{4,5},{5,4},{6,7},{7,6},{8,9},{9,8},{10,11... | collective-permute-start | bytes 2359304 | tf_op jit(solution)/shard_map/ppermute | solution.py:360
  46.4 4.9 %collective-permute-start.4 = (bf16[192,2048]{1,0:T(8,128)(2,1)}, bf16[192,2048]{1,0:T(8,128)(2,1)}, u32[]{:S(2)}, u32[]{:S(2)}) collective-permute-start(bf16[192,2048]{1,0:T(8,128)(2,1)} %collective-permute-done.3.refs_7_), channel_id=1, source_target_pairs={{0,4},{1,13},{2,6},{3,15},{4,8},{5,1},{6,10},{7,3},{8,12},{9,5},{1... | collective-permute-start | bytes 2359304 | tf_op jit(solution)/shard_map/ppermute | solution.py:359
  51.3 0.0 copy-done.2
  51.3 0.0 copy-done.3
  51.3 4.7 %all-to-all-done = bf16[8,16,768]{2,1,0:T(8,128)(2,1)S(1)} async-done(((bf16[8,16,768]{2,1,0:T(8,128)(2,1)}), bf16[8,16,768]{2,1,0:T(8,128)(2,1)S(1)}, u32[]{:S(2)}, u32[]{:S(2)}) %all-to-all-start) | async-done | bytes 196640 | tf_op jit(solution)/shard_map/all_to_all | solution.py:306
  56.0 10.9 %all_gather.7.all_ref = bf16[4,128,768]{2,1,0:T(8,128)(2,1)S(1)} all-gather(bf16[1,128,768]{2,1,0:T(8,128)(2,1)S(1)} %bitcast.9), channel_id=1, replica_groups={{0,16,272,256},{32,48,304,288},{64,80,336,320},{96,112,368,352},{128,14..., dimensions={0}, use_global_device_ids=true | all-gather | bytes 983040 | tf_op jit(solution)/shard_map/all_gather | solution.py:363
  66.9 0.0 collective-permute-done.2.refs_4_
  66.9 0.0 collective-permute-done.1.refs_3_
  66.9 0.0 collective-permute-done.5.refs_9_
  66.9 0.0 collective-permute-done.4.refs_8_
  66.9 8.9 %rows.1 = bf16[128,768]{1,0:T(8,128)(2,1)S(1)} custom-call(bf16[4,128,768]{2,1,0:T(8,128)(2,1)S(1)} %all_gather.7.all_ref, f32[1,768]{1,0:T(1,128)S(1)} %reshape.13.gain1_ref, f32[1,768]{1,0:T(1,128)S(1)} %reshape.14.gain2_ref, bf16[192,1536]{1,0:T(8,128)(2,1)} %refs_0_.3, bf16[192,512]{1,0:T(8,128)(2,1)} %bitcast.11, ...), custom_call_target="tpu_custom_call" | custom-call | flops 1140850688 | bytes 3932160 | tf_op jit(solution)/shard_map/rows/pallas_call | solution.py:283
  75.9 28.7 %all_to_all.10 = bf16[8,16,768]{2,1,0:T(8,128)(2,1)S(1)} all-to-all(bf16[8,16,768]{2,1,0:T(8,128)(2,1)S(1)} %bitcast.7), channel_id=1, replica_groups={{0,32,64,96,128,160,192,224},{16,48,80,112,144,176,208,240},{256,288,32..., dimensions={0} | all-to-all | bytes 393216 | tf_op jit(solution)/shard_map/all_to_all | solution.py:306
  104.5 0.7 copy.12
  (2 shorter events, 0.0 us)
Async XLA Ops:
  0.0 25.0 %copy-start = (bf16[768,1536]{1,0:T(8,128)(2,1)S(1)}, bf16[768,1536]{1,0:T(8,128)(2,1)}, u32[]{:S(2)}) copy-start(bf16[768,1536]{1,0:T(8,128)(2,1)} %weight_ref.1) | copy-start | bytes 7077892
  0.0 25.0 %copy-start.1 = (f32[768]{0:T(1024)S(1)}, f32[768]{0:T(1024)}, u32[]{:S(2)}) copy-start(f32[768]{0:T(1024)} %gain_ref.1) | copy-start | bytes 9220
  18.4 32.9 %copy-start.2 = (f32[768]{0:T(1024)S(1)}, f32[768]{0:T(1024)}, u32[]{:S(2)}) copy-start(f32[768]{0:T(1024)} %param.14) | copy-start | bytes 9220
  18.4 32.9 %copy-start.3 = (f32[768]{0:T(1024)S(1)}, f32[768]{0:T(1024)}, u32[]{:S(2)}) copy-start(f32[768]{0:T(1024)} %param.17) | copy-start | bytes 9220
  18.5 21.7 %collective-permute-start = (bf16[192,2048]{1,0:T(8,128)(2,1)S(1)}, bf16[192,2048]{1,0:T(8,128)(2,1)S(1)}, u32[]{:S(2)}, u32[]{:S(2)}) collective-permute-start(bf16[192,2048]{1,0:T(8,128)(2,1)S(1)} %get-tuple-element.13), channel_id=1, source_target_pairs={{0,4},{1,13},{2,6},{3,15},{4,8},{5,1},{6,10},{7,3},{8,12},{9,5},{1... | collective-permute-start | bytes 2359304 | tf_op jit(solution)/shard_map/ppermute | solution.py:356
  23.0 21.0 %collective-permute-start.3 = (bf16[192,2048]{1,0:T(8,128)(2,1)S(1)}, bf16[192,2048]{1,0:T(8,128)(2,1)}, u32[]{:S(2)}, u32[]{:S(2)}) collective-permute-start(bf16[192,2048]{1,0:T(8,128)(2,1)S(1)} %get-tuple-element.14), channel_id=1, source_target_pairs={{0,4},{1,13},{2,6},{3,15},{4,8},{5,1},{6,10},{7,3},{8,12},{9,5},{1... | collective-permute-start | bytes 2359304 | tf_op jit(solution)/shard_map/ppermute | solution.py:356
  28.1 27.9 %all-to-all-start = ((bf16[8,16,768]{2,1,0:T(8,128)(2,1)}), bf16[8,16,768]{2,1,0:T(8,128)(2,1)S(1)}, u32[]{:S(2)}, u32[]{:S(2)}) async-start(bf16[8,16,768]{2,1,0:T(8,128)(2,1)} %bitcast.3), calls=%async_computation | async-start | bytes 393216 | tf_op jit(solution)/shard_map/all_to_all | solution.py:306
  40.2 26.8 %collective-permute-start.2 = (bf16[192,2048]{1,0:T(8,128)(2,1)S(1)}, bf16[192,2048]{1,0:T(8,128)(2,1)S(1)}, u32[]{:S(2)}, u32[]{:S(2)}) collective-permute-start(bf16[192,2048]{1,0:T(8,128)(2,1)S(1)} %collective-permute-done.refs_2_), channel_id=1, source_target_pairs={{0,1},{1,0},{2,3},{3,2},{4,5},{5,4},{6,7},{7,6},{8,9},{9,8},{10,11... | collective-permute-start | bytes 2359304 | tf_op jit(solution)/shard_map/ppermute | solution.py:360
  42.1 24.8 %collective-permute-start.1 = (bf16[192,2048]{1,0:T(8,128)(2,1)S(1)}, bf16[192,2048]{1,0:T(8,128)(2,1)S(1)}, u32[]{:S(2)}, u32[]{:S(2)}) collective-permute-start(bf16[192,2048]{1,0:T(8,128)(2,1)S(1)} %collective-permute-done.refs_2_), channel_id=1, source_target_pairs={{0,4},{1,13},{2,6},{3,15},{4,8},{5,1},{6,10},{7,3},{8,12},{9,5},{1... | collective-permute-start | bytes 2359304 | tf_op jit(solution)/shard_map/ppermute | solution.py:359
  44.0 22.9 %collective-permute-start.5 = (bf16[192,2048]{1,0:T(8,128)(2,1)}, bf16[192,2048]{1,0:T(8,128)(2,1)}, u32[]{:S(2)}, u32[]{:S(2)}) collective-permute-start(bf16[192,2048]{1,0:T(8,128)(2,1)} %collective-permute-done.3.refs_7_), channel_id=1, source_target_pairs={{0,1},{1,0},{2,3},{3,2},{4,5},{5,4},{6,7},{7,6},{8,9},{9,8},{10,11... | collective-permute-start | bytes 2359304 | tf_op jit(solution)/shard_map/ppermute | solution.py:360
  46.4 20.5 %collective-permute-start.4 = (bf16[192,2048]{1,0:T(8,128)(2,1)}, bf16[192,2048]{1,0:T(8,128)(2,1)}, u32[]{:S(2)}, u32[]{:S(2)}) collective-permute-start(bf16[192,2048]{1,0:T(8,128)(2,1)} %collective-permute-done.3.refs_7_), channel_id=1, source_target_pairs={{0,4},{1,13},{2,6},{3,15},{4,8},{5,1},{6,10},{7,3},{8,12},{9,5},{1... | collective-permute-start | bytes 2359304 | tf_op jit(solution)/shard_map/ppermute | solution.py:359
